TPU v7x, 32 devices: a whole 2x2x4 slice. The times are simulated.
32 devices in a mesh: row: 4 (over y, x), col: 8 (over z, core).
Axes of the slice: x: 2, y: 2, z: 4, core: 2. Of those that a mesh axis runs over, the one named last changes fastest.
Arguments:
- inverses: bfloat16 [4, 32, 1024, 1024], P('row', 'col'), as said below
- coupling: bfloat16 [4, 32, 1024, 256], P('row', 'col'), may hold values from -0.1875 to 0.1875
- orders: int32 [4, 32], P('row', 'col'), may hold values from 512 to 1024, as said below
- owners: int32 [4, 32, 1], P(None, 'col'), may hold values from 0 to 3, as said below
- offsets: int32 [4, 32, 2], P(None, 'col'), may hold values from 0 to 2
- dense_slab: float32 [2048, 4096], P('row', 'col'), may hold values from -6 to 6
- pivots: float32 [1024], replicated, may hold values from 16 to 128
Outputs:
- result: float32 [2048, 4096], P('row', 'col')
Inputs may be any that keep to these rules, and one draw needn't show every extreme that they name: `orders`: order of each subdomain; some subdomain has exactly 1024. `owners`: within the 4 subdomains of one device (entries r, s with the same r and the same s // 4) no row block is named twice. `inverses`: each inverse is symmetric.
All inputs are finite; a program needn't handle non-finite values.
Results may differ from a plain program's by a relative error of at most 0.0035.
Values may be sent and summed in bfloat16 or wider, within the bound.
A program may use at most 64 MiB of HBM per device.

v0:
```python
import jax
import jax.numpy as jnp
from jax import lax
from jax.sharding import PartitionSpec as P

CAP = 1


def spread(value, axis, source):
    kept = jnp.where(lax.axis_index(axis) == source, value, 0).astype(value.dtype)
    return lax.psum(kept, axis)


def place_tile(schur_sum, tile_value, weight, row_start, col_start):
    couple_width = tile_value.shape[0]
    current = lax.dynamic_slice(schur_sum, (row_start, col_start), (couple_width, couple_width))
    return lax.dynamic_update_slice(
        schur_sum, current + weight * tile_value.astype(jnp.float32), (row_start, col_start)
    )


def body(inverses, coupling, orders, owners, offsets, dense_slab, pivots):
    sub_count = inverses.shape[1]
    order_size = inverses.shape[2]
    couple_width = coupling.shape[3]
    tile_size = dense_slab.shape[0]
    panel_width = pivots.shape[0]
    offset_unit = (tile_size - couple_width) // 2
    live_rows = jnp.arange(order_size, dtype=jnp.int32)[None, :, None] < orders[0][:, None, None]
    masked = jnp.where(live_rows, coupling[0], jnp.zeros_like(coupling[0]))
    solved = jnp.einsum(
        "sij,sjk->sik", inverses[0], masked, preferred_element_type=jnp.float32
    ).astype(jnp.bfloat16)
    schur_tiles = jnp.einsum(
        "sji,sjk->sik", masked, solved, preferred_element_type=jnp.float32
    ).astype(jnp.bfloat16)
    my_row = lax.axis_index("row")
    targets = owners[:, :, 0].reshape(-1)
    row_starts = offsets[:, :, 0].reshape(-1) * offset_unit
    col_starts = offsets[:, :, 1].reshape(-1) * offset_unit
    zero_sum = jnp.zeros((tile_size, tile_size), jnp.float32)
    row_count = lax.axis_size("row")
    grouped = targets.reshape(row_count, sub_count)
    same_owner = grouped[:, :, None] == grouped[:, None, :]
    earlier = jnp.arange(sub_count)[None, :] < jnp.arange(sub_count)[:, None]
    slot_rank = jnp.sum((same_owner & earlier[None]).astype(jnp.int32), axis=2).reshape(-1)
    my_targets = lax.dynamic_slice_in_dim(targets, my_row * sub_count, sub_count)
    my_ranks = lax.dynamic_slice_in_dim(slot_rank, my_row * sub_count, sub_count)
    slot_ids = my_targets * CAP + my_ranks
    selector = (slot_ids[:, None] == jnp.arange(row_count * CAP, dtype=jnp.int32)[None, :]).astype(
        jnp.bfloat16
    )
    flat_tiles = schur_tiles.reshape(sub_count, couple_width * couple_width)
    send_slots = jnp.dot(selector.T, flat_tiles, preferred_element_type=jnp.float32).astype(
        jnp.bfloat16
    )
    send_slots = send_slots.reshape(row_count, CAP, couple_width, couple_width)
    received = lax.all_to_all(send_slots, "row", split_axis=0, concat_axis=0, tiled=True)

    def one_slot(position, running):
        source = position // sub_count
        weight = (targets[position] == my_row).astype(jnp.float32)
        tile_value = received[source, jnp.minimum(slot_rank[position], CAP - 1)]
        return place_tile(running, tile_value, weight, row_starts[position], col_starts[position])

    schur_sum = lax.fori_loop(0, targets.shape[0], one_slot, zero_sum)
    updated = dense_slab - schur_sum
    rounded = updated.astype(jnp.bfloat16)
    panel_parts = []
    for part_index in range(panel_width // tile_size):
        panel_parts.append(spread(rounded, "row", part_index))
    panel_cols = jnp.concatenate(panel_parts, axis=0)
    crossed = spread(panel_cols, "col", lax.axis_index("row"))
    left_factor = (crossed.astype(jnp.float32) / pivots[:, None]).astype(jnp.bfloat16)
    update = lax.dot_general(
        left_factor, panel_cols, (((0,), (0,)), ((), ())), preferred_element_type=jnp.float32
    )
    return updated - update


def solution(mesh):
    placed = (
        P("row", "col", None, None),
        P("row", "col", None, None),
        P("row", "col"),
        P(None, "col", None),
        P(None, "col", None),
        P("row", "col"),
        P(),
    )
    return jax.shard_map(
        body, mesh=mesh, in_specs=placed, out_specs=P("row", "col"), check_vma=False
    )
```

profile of v0, /device:TPU:0, one launch (start us, length us, event | category | flops | bytes accessed | tf_op | source)
XLA Modules:
  0.0 318.1 jit_solution(6392637798119528049)
XLA Ops:
  6.5 1.0 convert_reduce_fusion
  8.1 1.3 reduce.11
  9.5 0.7 iota_compare_fusion
  10.3 7.5 %fusion.13 = bf16[1,4,256,256]{3,2,1,0:T(8,128)(2,1)S(1)} fusion(bf16[1,4,1024,1024]{3,2,1,0:T(8,128)(2,1)} %param.9, bf16[1,4,1024,256]{3,2,1,0:T(8,128)(2,1)} %param.10, pred[4,1024]{1,0:T(4,128)(4,1)S(1)} %iota_compare_fusion), kind=kOutput, calls=%fused_computation.10 | convolution fusion | flops 2687762432 | bytes 11014144 | tf_op jit(solution)/shard_map/sji,sjk->sik/dot_general | solution.py:34
  18.9 0.9 copy.20
  19.7 5.2 %all-to-all-start = ((bf16[4,1,256,256]{3,2,1,0:T(8,128)(2,1)}), bf16[4,1,256,256]{3,2,1,0:T(8,128)(2,1)S(1)}, u32[]{:S(2)}, u32[]{:S(2)}) async-start(bf16[4,1,256,256]{3,2,1,0:T(8,128)(2,1)} %bitcast.48), calls=%async_computation | async-start | bytes 1048576 | tf_op jit(solution)/shard_map/all_to_all | solution.py:58
  25.1 7.8 %all-to-all-done = bf16[4,1,256,256]{3,2,1,0:T(8,128)(2,1)S(1)} async-done(((bf16[4,1,256,256]{3,2,1,0:T(8,128)(2,1)}), bf16[4,1,256,256]{3,2,1,0:T(8,128)(2,1)S(1)}, u32[]{:S(2)}, u32[]{:S(2)}) %all-to-all-start) | async-done | bytes 524320 | tf_op jit(solution)/shard_map/all_to_all | solution.py:58
  33.1 157.7 %while.15 = (s32[]{:T(128)}, f32[512,512]{1,0:T(8,128)S(1)}, s32[16]{0:T(128)S(1)}, s32[16]{0:T(128)S(1)}, s32[16]{0:T(128)S(1)}, /*index=5*/s32[]{:T(128)}, bf1...) while((s32[]{:T(128)}, f32[512,512]{1,0:T(8,128)S(1)}, ...), condition=%wide.region_2.3_spmd, body=%wide.region_1.2_spmd.sunk | while | flops 196629 | bytes 1180039 | solution.py:66
  39.6 2.1 dynamic_update_slice.11
  48.2 4.7 %dynamic_update_slice.11 = f32[512,512]{1,0:T(8,128)S(1)} dynamic-update-slice(f32[512,512]{1,0:T(8,128)S(1)} %get-tuple-element.272, f32[256,256]{1,0:T(8,128)S(1)} %bitcast_add_fusion.2, s32[]{:T(128)S(6)} %select_n.121, s32[]{:T(128)S(6)} %select_n.122) | dynamic-update-slice | bytes 524292 | tf_op jit(solution)/shard_map/while/body/eval_jaxpr/dynamic_update_slice | solution.py:17
  59.4 4.7 %dynamic_update_slice.11 = f32[512,512]{1,0:T(8,128)S(1)} dynamic-update-slice(f32[512,512]{1,0:T(8,128)S(1)} %get-tuple-element.272, f32[256,256]{1,0:T(8,128)S(1)} %bitcast_add_fusion.2, s32[]{:T(128)S(6)} %select_n.121, s32[]{:T(128)S(6)} %select_n.122) | dynamic-update-slice | bytes 524292 | tf_op jit(solution)/shard_map/while/body/eval_jaxpr/dynamic_update_slice | solution.py:17
  70.6 3.0 dynamic_update_slice.11
  80.0 3.0 dynamic_update_slice.11
  89.5 2.6 dynamic_update_slice.11
  98.6 2.1 dynamic_update_slice.11
  107.2 3.3 %dynamic_update_slice.11 = f32[512,512]{1,0:T(8,128)S(1)} dynamic-update-slice(f32[512,512]{1,0:T(8,128)S(1)} %get-tuple-element.272, f32[256,256]{1,0:T(8,128)S(1)} %bitcast_add_fusion.2, s32[]{:T(128)S(6)} %select_n.121, s32[]{:T(128)S(6)} %select_n.122) | dynamic-update-slice | bytes 524292 | tf_op jit(solution)/shard_map/while/body/eval_jaxpr/dynamic_update_slice | solution.py:17
  116.9 4.7 %dynamic_update_slice.11 = f32[512,512]{1,0:T(8,128)S(1)} dynamic-update-slice(f32[512,512]{1,0:T(8,128)S(1)} %get-tuple-element.272, f32[256,256]{1,0:T(8,128)S(1)} %bitcast_add_fusion.2, s32[]{:T(128)S(6)} %select_n.121, s32[]{:T(128)S(6)} %select_n.122) | dynamic-update-slice | bytes 524292 | tf_op jit(solution)/shard_map/while/body/eval_jaxpr/dynamic_update_slice | solution.py:17
  128.1 3.9 %dynamic_update_slice.11 = f32[512,512]{1,0:T(8,128)S(1)} dynamic-update-slice(f32[512,512]{1,0:T(8,128)S(1)} %get-tuple-element.272, f32[256,256]{1,0:T(8,128)S(1)} %bitcast_add_fusion.2, s32[]{:T(128)S(6)} %select_n.121, s32[]{:T(128)S(6)} %select_n.122) | dynamic-update-slice | bytes 524292 | tf_op jit(solution)/shard_map/while/body/eval_jaxpr/dynamic_update_slice | solution.py:17
  138.5 3.3 %dynamic_update_slice.11 = f32[512,512]{1,0:T(8,128)S(1)} dynamic-update-slice(f32[512,512]{1,0:T(8,128)S(1)} %get-tuple-element.272, f32[256,256]{1,0:T(8,128)S(1)} %bitcast_add_fusion.2, s32[]{:T(128)S(6)} %select_n.121, s32[]{:T(128)S(6)} %select_n.122) | dynamic-update-slice | bytes 524292 | tf_op jit(solution)/shard_map/while/body/eval_jaxpr/dynamic_update_slice | solution.py:17
  148.3 3.0 dynamic_update_slice.11
  157.8 3.3 %dynamic_update_slice.11 = f32[512,512]{1,0:T(8,128)S(1)} dynamic-update-slice(f32[512,512]{1,0:T(8,128)S(1)} %get-tuple-element.272, f32[256,256]{1,0:T(8,128)S(1)} %bitcast_add_fusion.2, s32[]{:T(128)S(6)} %select_n.121, s32[]{:T(128)S(6)} %select_n.122) | dynamic-update-slice | bytes 524292 | tf_op jit(solution)/shard_map/while/body/eval_jaxpr/dynamic_update_slice | solution.py:17
  167.6 3.0 dynamic_update_slice.11
  177.0 2.6 dynamic_update_slice.11
  186.1 4.7 %dynamic_update_slice.11 = f32[512,512]{1,0:T(8,128)S(1)} dynamic-update-slice(f32[512,512]{1,0:T(8,128)S(1)} %get-tuple-element.272, f32[256,256]{1,0:T(8,128)S(1)} %bitcast_add_fusion.2, s32[]{:T(128)S(6)} %select_n.121, s32[]{:T(128)S(6)} %select_n.122) | dynamic-update-slice | bytes 524292 | tf_op jit(solution)/shard_map/while/body/eval_jaxpr/dynamic_update_slice | solution.py:17
  190.8 1.0 broadcast_select_fusion.1
  191.9 0.9 broadcast_select_fusion.2
  192.8 52.6 %all-reduce.6.cloned.1.call-done = (bf16[512,512]{1,0:T(8,128)(2,1)}, bf16[512,512]{1,0:T(8,128)(2,1)}) async-done(((bf16[512,512]{1,0:T(8,128)(2,1)}, bf16[512,512]{1,0:T(8,128)(2,1)}), (bf16[512,512]{1,0:T(8,128)(2,1)}, bf16[512,512]{1,0:T(8,128)(2,1)})) %all-reduce.6.cloned.1.call-update) | async-done | bytes 1048592 | tf_op jit(solution)/shard_map/psum | solution.py:11
  245.4 1.1 constant_dynamic-update-slice_fusion.1
  246.5 1.1 constant_dynamic-update-slice_fusion
  247.6 1.0 broadcast_select_fusion
  248.7 59.5 %all-reduce.4.cloned.1.call-done = bf16[1024,512]{1,0:T(8,128)(2,1)} async-done(((bf16[1024,512]{1,0:T(8,128)(2,1)}), bf16[1024,512]{1,0:T(8,128)(2,1)}) %all-reduce.4.cloned.1.call-update) | async-done | bytes 1048592 | tf_op jit(solution)/shard_map/psum | solution.py:11
  308.1 3.1 convolution_subtract_fusion
  (85 shorter events, 32.8 us)
Async XLA Ops:
  17.8 7.2 %copy-start.1 = (s32[4,4,2]{1,2,0:T(2,128)S(1)}, s32[4,4,2]{1,2,0:T(2,128)}, u32[]{:S(2)}) copy-start(s32[4,4,2]{1,2,0:T(2,128)} %param.13) | copy-start | bytes 388
  19.7 13.2 %all-to-all-start = ((bf16[4,1,256,256]{3,2,1,0:T(8,128)(2,1)}), bf16[4,1,256,256]{3,2,1,0:T(8,128)(2,1)S(1)}, u32[]{:S(2)}, u32[]{:S(2)}) async-start(bf16[4,1,256,256]{3,2,1,0:T(8,128)(2,1)} %bitcast.48), calls=%async_computation | async-start | bytes 1048576 | tf_op jit(solution)/shard_map/all_to_all | solution.py:58
  24.9 220.5 %all-reduce.6.cloned.1.call-start = ((), (), s32[]{:S(2)}) async-start(), calls=%async_computation.2 | async-start | bytes 2097152 | tf_op jit(solution)/shard_map/psum | solution.py:11
  33.1 157.7 %copy-start = (f32[512,512]{1,0:T(8,128)S(1)}, f32[512,512]{1,0:T(8,128)}, u32[]{:S(2)}) copy-start(f32[512,512]{1,0:T(8,128)} %param.14) | copy-start | bytes 3145732
  192.8 115.4 %all-reduce.4.cloned.1.call-start = ((), (), s32[]{:S(2)}) async-start(), calls=%async_computation.1 | async-start | bytes 2097152 | tf_op jit(solution)/shard_map/psum | solution.py:11
  246.5 61.6 %copy-start.2 = (f32[1024]{0:T(1024)S(1)}, f32[1024]{0:T(1024)}, u32[]{:S(2)}) copy-start(f32[1024]{0:T(1024)} %param.15) | copy-start | bytes 12292
Sparse Core Ops, SparseCore 0:
  192.9 52.4 all-reduce.5
  248.8 59.2 all-reduce.3
where the time goes:
time: 320 us; the launch traced here: 318 us
  waiting for transfers between devices  120 us (38%)
  local copies, waits for them, and re-layouts  86.3 us (27%)
  loops' own time  73.4 us (23%)
  between operations  13.5 us (4%)
  matrix products  11.2 us (4%)
  other arithmetic  8.52 us (3%)
  starting transfers between devices  5.23 us (2%)
    psum x2, waiting for transfers between devices, spread(): return lax.psum(kept, axis)  112 us
    another operation x1, loops' own time, body(): schur_sum = lax.fori_loop(0, targets.shape[0], one_slot, zero_sum)  73.4 us
    dynamic_update_slice x16, local copies, waits for them, and re-layouts, place_tile(): lax.dynamic_update_slice(schur_sum, current + weight * tile_value.astype(...  53.7 us
    dynamic_slice x16, local copies, waits for them, and re-layouts, one_slot(): weight = (targets[position] == my_row).astype(jnp.float32)  9.42 us
    dynamic_slice x16, local copies, waits for them, and re-layouts, one_slot(): col_starts[position]  9.41 us
    dynamic_slice x16, local copies, waits for them, and re-layouts, one_slot(): row_starts[position]  9.39 us
    all_to_all x1, waiting for transfers between devices, body(): lax.all_to_all(send_slots, 'row', split_axis=0, concat_axis=0, tiled=True)  7.82 us
    dot_general x1, matrix products, body(): jnp.einsum('sji,sjk->sik', masked, solved, preferred_element_type=jnp.flo...  7.49 us
  transfers between devices with their start and end apart: 3, of which 3 were waited for; matrix products, arithmetic and copies ran while one was open for 0% of the time, Pallas kernels for 0%

commit v1 on v0

v1 whole, which is shorter than its diff:
```python
import functools
import jax
import jax.numpy as jnp
from jax import lax
from jax.experimental import pallas as pl
from jax.experimental.pallas import tpu as pltpu
from jax.sharding import PartitionSpec as P

MESH = pl.DeviceIdType.MESH
BF16 = jnp.bfloat16
F32 = jnp.float32
CHUNKS = 8
GROUPS = 2
AB = 256


def contract0(a, b):
    return lax.dot_general(a, b, (((0,), (0,)), ((), ())), preferred_element_type=F32)


def kernel(
    dims,
    inv_hbm, cpl_hbm, orders, owners, offsets, slab_hbm, pivots,
    out,
    a_buf, m_buf, slab, mm, sol, tiles, send, recv, panel, left, piv,
    a_sem, m_sem, s_sem, t_send, t_recv, ax_send, ay_send, g_recv,
    up_send, dn_send, core_send, l_recv,
):
    rows, cols, subs, order, width, tile = dims
    unit = (tile - width) // 2
    nb = width // unit
    grid = tile // unit
    pairs = [(a, b) for a in range(nb) for b in range(a, nb)]
    upper = len(pairs)
    chunk = tile // CHUNKS
    ablocks = order // AB

    r = lax.axis_index("row")
    c = lax.axis_index("col")
    q, core = lax.div(c, 2), lax.rem(c, 2)
    chips = cols // 2
    q0, k0 = lax.div(r, 2), lax.rem(r, 2)
    pa = lax.rem(r, 2)
    pb = 1 - pa
    mate = r + 1 - 2 * pa
    on_line = core == k0
    diag = (q == q0) & on_line
    has_up = on_line & (q >= q0) & (q + 1 < chips)
    has_dn = on_line & (q <= q0) & (q > 0)
    hops = jnp.where(q >= q0, q - q0, q0 - q) + jnp.where(on_line, 0, 1)

    def load_a(s, i):
        return pltpu.make_async_copy(
            inv_hbm.at[0, s, pl.ds(i * AB, AB), pl.ds(i * AB, order - i * AB)],
            a_buf.at[s, pl.ds(i * AB, AB), pl.ds(i * AB, order - i * AB)],
            a_sem.at[s, i])

    def load_m(s):
        return pltpu.make_async_copy(cpl_hbm.at[0, s], m_buf.at[s], m_sem.at[s])

    load_slab = pltpu.make_async_copy(slab_hbm, slab, s_sem)
    for s in range(subs):
        load_m(s).start()
        for i in range(ablocks):
            load_a(s, i).start()
    load_slab.start()

    barrier = pltpu.get_barrier_semaphore()
    for t in range(rows):
        @pl.when(t != r)
        def _():
            pl.semaphore_signal(barrier, inc=1, device_id=(t, c), device_id_type=MESH)
    pl.semaphore_signal(barrier, inc=1, device_id=(r, c + 1 - 2 * core), device_id_type=MESH)

    @pl.when(q + 1 < chips)
    def _():
        pl.semaphore_signal(barrier, inc=1, device_id=(r, c + 2), device_id_type=MESH)

    @pl.when(q > 0)
    def _():
        pl.semaphore_signal(barrier, inc=1, device_id=(r, c - 2), device_id_type=MESH)

    for k in range(pivots.shape[0]):
        piv[pl.ds(k * 128, 128), :] = jnp.transpose(
            jnp.broadcast_to(pivots[pl.ds(k, 1), :], (128, 128)))
    for t in range(rows):
        recv[t, nb * nb] = jnp.zeros((unit, unit), BF16)

    for s in range(subs):
        load_m(s).wait()
        live = lax.broadcasted_iota(jnp.int32, (order, width), 0) < orders[0, s]
        mm[...] = jnp.where(live, m_buf[s], jnp.zeros((order, width), BF16))
        for i in range(ablocks):
            load_a(s, i).wait()
            lo = i * AB
            half = a_buf[s, lo:lo + AB, lo:lo + AB] * jnp.asarray(0.5, BF16)
            part = jnp.dot(half, mm[lo:lo + AB], preferred_element_type=F32)
            if i + 1 < ablocks:
                part = part + jnp.dot(a_buf[s, lo:lo + AB, lo + AB:], mm[lo + AB:],
                                      preferred_element_type=F32)
            sol[lo:lo + AB] = part.astype(BF16)
        half_tile = contract0(mm[...], sol[...])
        whole_tile = (half_tile + jnp.transpose(half_tile)).astype(BF16)
        for k, (a, b) in enumerate(pairs):
            tiles[s, k] = whole_tile[a * unit:(a + 1) * unit, b * unit:(b + 1) * unit]

    neighbours = rows + jnp.where(q + 1 < chips, 1, 0) + jnp.where(q > 0, 1, 0)
    pl.semaphore_wait(barrier, neighbours)

    def pick(src, dst):
        found, which = jnp.int32(0), jnp.int32(0)
        for s in range(subs):
            hit = owners[src, s, 0] == dst
            found, which = jnp.where(hit, 1, found), jnp.where(hit, s, which)
        return found, which

    def tile_copy(t, src_row):
        return pltpu.make_async_remote_copy(
            src_ref=send.at[t], dst_ref=recv.at[src_row, pl.ds(0, upper)],
            send_sem=t_send.at[t], recv_sem=t_recv.at[src_row],
            device_id=(t, c), device_id_type=MESH)

    for t in range(rows):
        _, which = pick(r, t)
        value = tiles[which]

        @pl.when(t != r)
        def _():
            send[t] = value
            tile_copy(t, r).start()

        @pl.when(t == r)
        def _():
            recv[t, pl.ds(0, upper)] = value

    def part(ref, p, j):
        return ref.at[p, pl.ds(pl.multiple_of(j * chunk, chunk), chunk)]

    def panel_copy(j, target, sems):
        return pltpu.make_async_remote_copy(
            src_ref=part(panel, pa, j), dst_ref=part(panel, pa, j),
            send_sem=sems.at[j], recv_sem=g_recv.at[pa, j],
            device_id=(target, c), device_id_type=MESH)

    def panel_got(p, j):
        pltpu.make_async_remote_copy(
            src_ref=part(panel, p, j), dst_ref=part(panel, p, j),
            send_sem=ax_send.at[j], recv_sem=g_recv.at[p, j],
            device_id=(mate, c), device_id_type=MESH).wait_recv()

    def send_panel(j):
        @pl.when(r + 2 < rows)
        def _():
            panel_copy(j, r + 2, ay_send).start()
        panel_copy(j, mate, ax_send).start()

    def left_copy(src, p, j, target, sems):
        return pltpu.make_async_remote_copy(
            src_ref=part(src, p, j), dst_ref=part(left, p, j),
            send_sem=sems.at[p, j], recv_sem=l_recv.at[p, j],
            device_id=(r, target), device_id_type=MESH)

    def forward(src, p, j):
        @pl.when(has_up)
        def _():
            left_copy(src, p, j, c + 2, up_send).start()

        @pl.when(has_dn)
        def _():
            left_copy(src, p, j, c - 2, dn_send).start()
        left_copy(src, p, j, c + 1 - 2 * core, core_send).start()

    load_slab.wait()
    places = []
    for t in range(rows):
        found, which = pick(t, r)
        places.append((found, offsets[t, which, 0], offsets[t, which, 1]))

        @pl.when(t != r)
        def _():
            tile_copy(t, t).wait_recv()
    low = [(a, b) for a in range(nb) for b in range(a)]
    for t in range(rows):
        for k, (a, b) in enumerate(low):
            mirror = recv[t, pairs.index((b, a))].astype(F32)
            recv[t, upper + k] = jnp.transpose(mirror).astype(BF16)
    slots = {pair: k for k, pair in enumerate(pairs + low)}
    for i in range(grid):
        for j in range(grid):
            block = slab[i * unit:(i + 1) * unit, j * unit:(j + 1) * unit]
            total = jnp.zeros((unit, unit), F32)
            for t in range(rows):
                found, at_row, at_col = places[t]
                slot = jnp.int32(nb * nb)
                for (a, b), k in slots.items():
                    here = (found > 0) & (at_row + a == i) & (at_col + b == j)
                    slot = jnp.where(here, k, slot)
                total = total + recv[t, slot].astype(F32)
            out[i * unit:(i + 1) * unit, j * unit:(j + 1) * unit] = block - total

        @pl.when(r < 2)
        def _():
            span = slice(i * unit, (i + 1) * unit)
            panel[pa, span] = out[span, :].astype(BF16)
            for j in range(i * unit // chunk, (i + 1) * unit // chunk):
                send_panel(j)

    per_group = CHUNKS // GROUPS
    depth = per_group * chunk
    lanes = tile // 128

    def step(n, carry):
        @pl.when(n < CHUNKS)
        def _():
            @pl.when(r >= 2)
            def _():
                panel_got(pa, n)
                send_panel(n)

            @pl.when(diag)
            def _():
                forward(panel, pa, n)
            panel_got(pb, n)

            @pl.when(diag)
            def _():
                forward(panel, pb, n)
        j = n - hops

        @pl.when(j >= 0)
        def _():
            for p in (pa, pb):
                @pl.when(jnp.logical_not(diag))
                def _():
                    left_copy(left, p, j, c + 1 - 2 * core, core_send).wait_recv()

                    @pl.when(on_line)
                    def _():
                        forward(left, p, j)

                @pl.when(diag)
                def _():
                    at = pl.ds(pl.multiple_of(j * chunk, chunk), chunk)
                    left[p, at] = panel[p, at]

            @pl.when(lax.rem(j, per_group) == per_group - 1)
            def _():
                first = pl.multiple_of((j - (per_group - 1)) * chunk, depth)
                total = jnp.zeros((tile, tile), F32)
                for p in range(2):
                    pivot = piv[pl.ds(pl.multiple_of(p * tile + first, depth), depth), :]
                    raw = left[p, pl.ds(first, depth)].astype(F32)
                    factor = (raw / jnp.concatenate([pivot] * lanes, axis=1)).astype(BF16)
                    total = total + contract0(factor, panel[p, pl.ds(first, depth)])
                out[...] = out[...] - total
        return carry

    lax.fori_loop(0, CHUNKS + hops, step, 0)

    for t in range(rows):
        @pl.when(t != r)
        def _():
            tile_copy(t, r).wait_send()

    def drain(j, carry):
        @pl.when(r + 2 < rows)
        def _():
            panel_copy(j, r + 2, ay_send).wait_send()
        panel_copy(j, mate, ax_send).wait_send()

        @pl.when(on_line)
        def _():
            for p in range(2):
                @pl.when(has_up)
                def _():
                    left_copy(left, p, j, c + 2, up_send).wait_send()

                @pl.when(has_dn)
                def _():
                    left_copy(left, p, j, c - 2, dn_send).wait_send()
                left_copy(left, p, j, c + 1 - 2 * core, core_send).wait_send()
        return carry

    lax.fori_loop(0, CHUNKS, drain, 0)


def body(rows, cols, inverses, coupling, orders, owners, offsets, dense_slab, pivots):
    subs, order = inverses.shape[1], inverses.shape[2]
    width, tile = coupling.shape[3], dense_slab.shape[0]
    unit = (tile - width) // 2
    nb = width // unit
    upper = nb * (nb + 1) // 2
    panel_width = pivots.shape[0]
    assert panel_width == 2 * tile and rows % 2 == 0 and cols % 2 == 0
    dma = pltpu.SemaphoreType.DMA
    hbm = pl.BlockSpec(memory_space=pl.ANY)
    smem = pl.BlockSpec(memory_space=pltpu.SMEM)
    vmem = pl.BlockSpec(memory_space=pltpu.VMEM)
    return pl.pallas_call(
        functools.partial(kernel, (rows, cols, subs, order, width, tile)),
        out_shape=jax.ShapeDtypeStruct((tile, tile), F32),
        in_specs=[hbm, hbm, smem, smem, smem, hbm, vmem],
        out_specs=vmem,
        scratch_shapes=[
            pltpu.VMEM((subs, order, order), BF16),
            pltpu.VMEM((subs, order, width), BF16),
            pltpu.VMEM((tile, tile), F32),
            pltpu.VMEM((order, width), BF16),
            pltpu.VMEM((order, width), BF16),
            pltpu.VMEM((subs, upper, unit, unit), BF16),
            pltpu.VMEM((rows, upper, unit, unit), BF16),
            pltpu.VMEM((rows, nb * nb + 1, unit, unit), BF16),
            pltpu.VMEM((2, tile, tile), BF16),
            pltpu.VMEM((2, tile, tile), BF16),
            pltpu.VMEM((panel_width, 128), F32),
            dma((subs, order // AB)), dma((subs,)), dma(()),
            dma((rows,)), dma((rows,)),
            dma((CHUNKS,)), dma((CHUNKS,)), dma((2, CHUNKS)),
            dma((2, CHUNKS)), dma((2, CHUNKS)), dma((2, CHUNKS)), dma((2, CHUNKS)),
        ],
        compiler_params=pltpu.CompilerParams(collective_id=0, has_side_effects=True),
    )(inverses, coupling, orders, owners, offsets, dense_slab, pivots.reshape(-1, 128))


def solution(mesh):
    placed = (
        P("row", "col", None, None),
        P("row", "col", None, None),
        P("row", "col"),
        P(None, "col", None),
        P(None, "col", None),
        P("row", "col"),
        P(),
    )
    return jax.shard_map(
        functools.partial(body, mesh.shape["row"], mesh.shape["col"]),
        mesh=mesh, in_specs=placed, out_specs=P("row", "col"), check_vma=False)
```

time: 320 us -> 62.9 us (0.20)
  the two profiles are of different devices: /device:TPU:0 before, /device:TPU:29 now
where the time goes in v1:
time: 62.9 us; the launch traced here: 62.6 us
  Pallas kernels  57.6 us (92%)
  local copies, waits for them, and re-layouts  5.01 us (8%)
    pallas_call x1, Pallas kernels, body(): pl.pallas_call(functools.partial(kernel, (rows, cols, subs, order, width,...  57.6 us
    unnamed x3, local copies, waits for them, and re-layouts  5.01 us

profile of v1, /device:TPU:29, one launch (start us, length us, event | category | flops | bytes accessed | tf_op | source)
XLA Modules:
  0.0 62.6 jit_solution(10003699703730509980)
XLA Ops:
  0.0 1.4 %copy.8.owners = s32[4,4,1]{2,1,0:T(4,128)} copy(s32[4,4,1]{1,2,0:T(1,128)} %param.10) | data formatting | bytes 128 | tf_op args[3]
  1.4 1.4 %copy.9.offsets = s32[4,4,2]{2,1,0:T(4,128)} copy(s32[4,4,2]{1,2,0:T(2,128)} %param.11) | data formatting | bytes 256 | tf_op args[4]
  2.8 57.6 %shard_map.73 = f32[512,512]{1,0:T(8,128)} custom-call(bf16[1,4,1024,1024]{3,2,1,0:T(8,128)(2,1)} %inv_hbm.1, bf16[1,4,1024,256]{3,2,1,0:T(8,128)(2,1)} %cpl_hbm.1, s32[1,4]{1,0:T(1,128)} %orders.1, s32[4,4,1]{2,1,0:T(4,128)} %copy.8.owners, s32[4,4,2]{2,1,0:T(4,128)} %copy.9.offsets, f32[512,512]{1,0:T(8,128)} %slab_hbm.1, f32[8,128]{1,0:T(8,128)} %bitcast.1), custom_call_target="tpu_custom_call" | custom-call | tf_op jit(solution)/shard_map/pallas_call | solution.py:299
  60.4 2.3 %copy.11 = f32[512,512]{1,0:T(8,128)} copy(f32[512,512]{1,0:T(8,128)} %shard_map.73) | data formatting | bytes 2097152

commit v2 on v1

--- a/solution.py
+++ b/solution.py
@@ -10,7 +10,6 @@
 BF16 = jnp.bfloat16
 F32 = jnp.float32
 CHUNKS = 8
-GROUPS = 2
 AB = 256
 
 
@@ -22,7 +21,7 @@
     dims,
     inv_hbm, cpl_hbm, orders, owners, offsets, slab_hbm, pivots,
     out,
-    a_buf, m_buf, slab, mm, sol, tiles, send, recv, panel, left, piv,
+    a_buf, m_buf, slab, mm, sol, tiles, send, recv, placed, panel, left, piv,
     a_sem, m_sem, s_sem, t_send, t_recv, ax_send, ay_send, g_recv,
     up_send, dn_send, core_send, l_recv,
 ):
@@ -31,7 +30,6 @@
     nb = width // unit
     grid = tile // unit
     pairs = [(a, b) for a in range(nb) for b in range(a, nb)]
-    upper = len(pairs)
     chunk = tile // CHUNKS
     ablocks = order // AB
 
@@ -47,7 +45,7 @@
     diag = (q == q0) & on_line
     has_up = on_line & (q >= q0) & (q + 1 < chips)
     has_dn = on_line & (q <= q0) & (q > 0)
-    hops = jnp.where(q >= q0, q - q0, q0 - q) + jnp.where(on_line, 0, 1)
+    chip_hops = jnp.where(q >= q0, q - q0, q0 - q)
 
     def load_a(s, i):
         return pltpu.make_async_copy(
@@ -84,7 +82,9 @@
         piv[pl.ds(k * 128, 128), :] = jnp.transpose(
             jnp.broadcast_to(pivots[pl.ds(k, 1), :], (128, 128)))
     for t in range(rows):
-        recv[t, nb * nb] = jnp.zeros((unit, unit), BF16)
+        for k in range(nb + 1):
+            placed[t, k * (nb + 1) + nb] = jnp.zeros((unit, unit), BF16)
+            placed[t, nb * (nb + 1) + k] = jnp.zeros((unit, unit), BF16)
 
     for s in range(subs):
         load_m(s).wait()
@@ -110,13 +110,13 @@
     def pick(src, dst):
         found, which = jnp.int32(0), jnp.int32(0)
         for s in range(subs):
-            hit = owners[src, s, 0] == dst
+            hit = owners[src, 0, s] == dst
             found, which = jnp.where(hit, 1, found), jnp.where(hit, s, which)
         return found, which
 
     def tile_copy(t, src_row):
         return pltpu.make_async_remote_copy(
-            src_ref=send.at[t], dst_ref=recv.at[src_row, pl.ds(0, upper)],
+            src_ref=send.at[t], dst_ref=recv.at[src_row],
             send_sem=t_send.at[t], recv_sem=t_recv.at[src_row],
             device_id=(t, c), device_id_type=MESH)
 
@@ -131,7 +131,7 @@
 
         @pl.when(t == r)
         def _():
-            recv[t, pl.ds(0, upper)] = value
+            recv[t] = value
 
     def part(ref, p, j):
         return ref.at[p, pl.ds(pl.multiple_of(j * chunk, chunk), chunk)]
@@ -172,31 +172,31 @@
 
     load_slab.wait()
     places = []
+    side = nb + 1
     for t in range(rows):
         found, which = pick(t, r)
-        places.append((found, offsets[t, which, 0], offsets[t, which, 1]))
+        at_row, at_col = offsets[t, 0, which], offsets[t, 1, which]
+        spots = []
+        for start in (at_row, at_col):
+            inside = [(found > 0) & (k - start >= 0) & (k - start < nb) for k in range(grid)]
+            spots.append([jnp.where(ok, k - start, nb) for k, ok in enumerate(inside)])
+        places.append(([side * a for a in spots[0]], spots[1]))
 
         @pl.when(t != r)
         def _():
             tile_copy(t, t).wait_recv()
-    low = [(a, b) for a in range(nb) for b in range(a)]
-    for t in range(rows):
-        for k, (a, b) in enumerate(low):
-            mirror = recv[t, pairs.index((b, a))].astype(F32)
-            recv[t, upper + k] = jnp.transpose(mirror).astype(BF16)
-    slots = {pair: k for k, pair in enumerate(pairs + low)}
+    for t in range(rows):
+        for k, (a, b) in enumerate(pairs):
+            value = recv[t, k]
+            placed[t, a * side + b] = value
+            if a != b:
+                placed[t, b * side + a] = jnp.transpose(value.astype(F32)).astype(BF16)
     for i in range(grid):
         for j in range(grid):
-            block = slab[i * unit:(i + 1) * unit, j * unit:(j + 1) * unit]
-            total = jnp.zeros((unit, unit), F32)
+            total = slab[i * unit:(i + 1) * unit, j * unit:(j + 1) * unit]
             for t in range(rows):
-                found, at_row, at_col = places[t]
-                slot = jnp.int32(nb * nb)
-                for (a, b), k in slots.items():
-                    here = (found > 0) & (at_row + a == i) & (at_col + b == j)
-                    slot = jnp.where(here, k, slot)
-                total = total + recv[t, slot].astype(F32)
-            out[i * unit:(i + 1) * unit, j * unit:(j + 1) * unit] = block - total
+                total = total - placed[t, places[t][0][i] + places[t][1][j]].astype(F32)
+            out[i * unit:(i + 1) * unit, j * unit:(j + 1) * unit] = total
 
         @pl.when(r < 2)
         def _():
@@ -205,57 +205,60 @@
             for j in range(i * unit // chunk, (i + 1) * unit // chunk):
                 send_panel(j)
 
-    per_group = CHUNKS // GROUPS
-    depth = per_group * chunk
     lanes = tile // 128
+    late = jnp.where(r >= 2, 2, 0)
+    first_left = jnp.where(diag, 0, lax.div(5 * chip_hops, 4) + jnp.where(on_line, 0, 1)
+                           + jnp.where(r >= 2, 1, 0))
 
     def step(n, carry):
-        @pl.when(n < CHUNKS)
-        def _():
-            @pl.when(r >= 2)
-            def _():
-                panel_got(pa, n)
-                send_panel(n)
-
+        @pl.when((n < CHUNKS) & (r >= 2))
+        def _():
+            panel_got(pa, n)
+            send_panel(n)
+
+        def own(p, j):
             @pl.when(diag)
             def _():
-                forward(panel, pa, n)
-            panel_got(pb, n)
-
-            @pl.when(diag)
+                forward(panel, p, j)
+                at = pl.ds(pl.multiple_of(j * chunk, chunk), chunk)
+                left[p, at] = panel[p, at]
+
+        def other(p, j):
+            @pl.when((j >= 0) & (j < CHUNKS) & jnp.logical_not(diag))
             def _():
-                forward(panel, pb, n)
-        j = n - hops
+                left_copy(left, p, j, c + 1 - 2 * core, core_send).wait_recv()
+
+                @pl.when(on_line)
+                def _():
+                    forward(left, p, j)
+
+        @pl.when(n < CHUNKS)
+        def _():
+            own(pa, n)
+        m = n - late
+
+        @pl.when((m >= 0) & (m < CHUNKS))
+        def _():
+            panel_got(pb, m)
+            own(pb, m)
+        other(pa, n - first_left)
+        j = m - first_left
+        other(pb, j)
 
         @pl.when(j >= 0)
         def _():
-            for p in (pa, pb):
-                @pl.when(jnp.logical_not(diag))
-                def _():
-                    left_copy(left, p, j, c + 1 - 2 * core, core_send).wait_recv()
-
-                    @pl.when(on_line)
-                    def _():
-                        forward(left, p, j)
-
-                @pl.when(diag)
-                def _():
-                    at = pl.ds(pl.multiple_of(j * chunk, chunk), chunk)
-                    left[p, at] = panel[p, at]
-
-            @pl.when(lax.rem(j, per_group) == per_group - 1)
-            def _():
-                first = pl.multiple_of((j - (per_group - 1)) * chunk, depth)
-                total = jnp.zeros((tile, tile), F32)
-                for p in range(2):
-                    pivot = piv[pl.ds(pl.multiple_of(p * tile + first, depth), depth), :]
-                    raw = left[p, pl.ds(first, depth)].astype(F32)
-                    factor = (raw / jnp.concatenate([pivot] * lanes, axis=1)).astype(BF16)
-                    total = total + contract0(factor, panel[p, pl.ds(first, depth)])
-                out[...] = out[...] - total
+            at = pl.ds(pl.multiple_of(j * chunk, chunk), chunk)
+            factors, rights = [], []
+            for p in range(2):
+                pivot = piv[pl.ds(pl.multiple_of(p * tile + j * chunk, chunk), chunk), :]
+                raw = left[p, at].astype(F32)
+                factors.append((raw / jnp.concatenate([pivot] * lanes, axis=1)).astype(BF16))
+                rights.append(panel[p, at])
+            factor = jnp.concatenate(factors, axis=0)
+            out[...] = out[...] - contract0(factor, jnp.concatenate(rights, axis=0))
         return carry
 
-    lax.fori_loop(0, CHUNKS + hops, step, 0)
+    lax.fori_loop(0, CHUNKS + first_left + late, step, 0)
 
     for t in range(rows):
         @pl.when(t != r)
@@ -298,7 +301,7 @@
     vmem = pl.BlockSpec(memory_space=pltpu.VMEM)
     return pl.pallas_call(
         functools.partial(kernel, (rows, cols, subs, order, width, tile)),
-        out_shape=jax.ShapeDtypeStruct((tile, tile), F32),
+        out_shape=pltpu.VMEM((tile, tile), F32),
         in_specs=[hbm, hbm, smem, smem, smem, hbm, vmem],
         out_specs=vmem,
         scratch_shapes=[
@@ -309,7 +312,8 @@
             pltpu.VMEM((order, width), BF16),
             pltpu.VMEM((subs, upper, unit, unit), BF16),
             pltpu.VMEM((rows, upper, unit, unit), BF16),
-            pltpu.VMEM((rows, nb * nb + 1, unit, unit), BF16),
+            pltpu.VMEM((rows, upper, unit, unit), BF16),
+            pltpu.VMEM((rows, (nb + 1) * (nb + 1), unit, unit), BF16),
             pltpu.VMEM((2, tile, tile), BF16),
             pltpu.VMEM((2, tile, tile), BF16),
             pltpu.VMEM((panel_width, 128), F32),
@@ -319,7 +323,8 @@
             dma((2, CHUNKS)), dma((2, CHUNKS)), dma((2, CHUNKS)), dma((2, CHUNKS)),
         ],
         compiler_params=pltpu.CompilerParams(collective_id=0, has_side_effects=True),
-    )(inverses, coupling, orders, owners, offsets, dense_slab, pivots.reshape(-1, 128))
+    )(inverses, coupling, orders, jnp.transpose(owners, (0, 2, 1)),
+      jnp.transpose(offsets, (0, 2, 1)), dense_slab, pivots.reshape(-1, 128))
 
 
 def solution(mesh):

time: 62.9 us -> 42.7 us (0.68)
  Pallas kernels: 57.6 us -> 41.3 us
  local copies, waits for them, and re-layouts: 5.01 us -> 0.97 us
    pallas_call x1, Pallas kernels: 57.6 us -> 41.3 us  [body(): pl.pallas_call(functools.partial(kernel, (rows, cols, subs, order, width,...]
    unnamed x3 -> x1, local copies, waits for them, and re-layouts: 5.01 us -> 0.97 us
where the time goes in v2:
time: 42.7 us; the launch traced here: 42.2 us
  Pallas kernels  41.3 us (97%)
  local copies, waits for them, and re-layouts  0.97 us (2%)
    pallas_call x1, Pallas kernels, body(): pl.pallas_call(functools.partial(kernel, (rows, cols, subs, order, width,...  41.3 us
    unnamed x1, local copies, waits for them, and re-layouts  0.97 us

profile of v2, /device:TPU:29, one launch (start us, length us, event | category | flops | bytes accessed | tf_op | source)
XLA Modules:
  0.0 42.2 jit_solution(11125430221310593315)
XLA Ops:
  0.0 41.3 %shard_map.73 = f32[512,512]{1,0:T(8,128)S(1)} custom-call(bf16[1,4,1024,1024]{3,2,1,0:T(8,128)(2,1)} %inv_hbm.1, bf16[1,4,1024,256]{3,2,1,0:T(8,128)(2,1)} %cpl_hbm.1, s32[1,4]{1,0:T(1,128)} %orders.1, s32[4,1,4]{2,1,0:T(1,128)} %bitcast.7, s32[4,2,4]{2,1,0:T(2,128)} %bitcast.5, f32[512,512]{1,0:T(8,128)} %slab_hbm.1, f32[8,128]{1,0:T(8,128)} %bitcast.6), custom_call_target="tpu_custom_call" | custom-call | tf_op jit(solution)/shard_map/pallas_call | solution.py:302
  41.3 1.0 %copy.10 = f32[512,512]{1,0:T(8,128)} copy(f32[512,512]{1,0:T(8,128)S(1)} %shard_map.73) | data formatting | bytes 2097152

commit v3 on v2

--- a/solution.py
+++ b/solution.py
@@ -9,7 +9,8 @@
 MESH = pl.DeviceIdType.MESH
 BF16 = jnp.bfloat16
 F32 = jnp.float32
-CHUNKS = 8
+CHUNKS = 16
+MERGE = 2
 AB = 256
 
 
@@ -206,9 +207,8 @@
                 send_panel(j)
 
     lanes = tile // 128
-    late = jnp.where(r >= 2, 2, 0)
-    first_left = jnp.where(diag, 0, lax.div(5 * chip_hops, 4) + jnp.where(on_line, 0, 1)
-                           + jnp.where(r >= 2, 1, 0))
+    late = 3
+    first_left = jnp.where(diag, 0, 2 * chip_hops + jnp.where(on_line, 0, 1))
 
     def step(n, carry):
         @pl.when((n < CHUNKS) & (r >= 2))
@@ -237,7 +237,7 @@
             own(pa, n)
         m = n - late
 
-        @pl.when((m >= 0) & (m < CHUNKS))
+        @pl.when((m >= 0) & (m < CHUNKS) & diag)
         def _():
             panel_got(pb, m)
             own(pb, m)
@@ -245,12 +245,17 @@
         j = m - first_left
         other(pb, j)
 
-        @pl.when(j >= 0)
-        def _():
-            at = pl.ds(pl.multiple_of(j * chunk, chunk), chunk)
+        @pl.when((j >= 0) & jnp.logical_not(diag))
+        def _():
+            panel_got(pb, j)
+
+        @pl.when((j >= 0) & (lax.rem(j, MERGE) == MERGE - 1))
+        def _():
+            first = pl.multiple_of((j - (MERGE - 1)) * chunk, MERGE * chunk)
+            at = pl.ds(first, MERGE * chunk)
             factors, rights = [], []
             for p in range(2):
-                pivot = piv[pl.ds(pl.multiple_of(p * tile + j * chunk, chunk), chunk), :]
+                pivot = piv[pl.ds(pl.multiple_of(p * tile + first, chunk), MERGE * chunk), :]
                 raw = left[p, at].astype(F32)
                 factors.append((raw / jnp.concatenate([pivot] * lanes, axis=1)).astype(BF16))
                 rights.append(panel[p, at])

time: 42.7 us -> 43.7 us (1.023)
  Pallas kernels: 41.3 us -> 42.6 us
    pallas_call x1, Pallas kernels: 41.3 us -> 42.6 us  [body(): pl.pallas_call(functools.partial(kernel, (rows, cols, subs, order, width,...]
where the time goes in v3:
time: 43.7 us; the launch traced here: 43.6 us
  Pallas kernels  42.6 us (97%)
  local copies, waits for them, and re-layouts  0.97 us (2%)
    pallas_call x1, Pallas kernels, body(): pl.pallas_call(functools.partial(kernel, (rows, cols, subs, order, width,...  42.6 us
    unnamed x1, local copies, waits for them, and re-layouts  0.97 us

profile of v3, /device:TPU:29, one launch (start us, length us, event | category | flops | bytes accessed | tf_op | source)
XLA Modules:
  0.0 43.6 jit_solution(5406996965775364361)
XLA Ops:
  0.0 42.6 %shard_map.73 = f32[512,512]{1,0:T(8,128)S(1)} custom-call(bf16[1,4,1024,1024]{3,2,1,0:T(8,128)(2,1)} %inv_hbm.1, bf16[1,4,1024,256]{3,2,1,0:T(8,128)(2,1)} %cpl_hbm.1, s32[1,4]{1,0:T(1,128)} %orders.1, s32[4,1,4]{2,1,0:T(1,128)} %bitcast.7, s32[4,2,4]{2,1,0:T(2,128)} %bitcast.5, f32[512,512]{1,0:T(8,128)} %slab_hbm.1, f32[8,128]{1,0:T(8,128)} %bitcast.6), custom_call_target="tpu_custom_call" | custom-call | tf_op jit(solution)/shard_map/pallas_call | solution.py:307
  42.6 1.0 %copy.10 = f32[512,512]{1,0:T(8,128)} copy(f32[512,512]{1,0:T(8,128)S(1)} %shard_map.73) | data formatting | bytes 2097152

commit v4 on v3

--- a/solution.py
+++ b/solution.py
@@ -207,8 +207,9 @@
                 send_panel(j)
 
     lanes = tile // 128
-    late = 3
-    first_left = jnp.where(diag, 0, 2 * chip_hops + jnp.where(on_line, 0, 1))
+    late = 4
+    off_line = jnp.where(on_line, 0, 2)
+    first_left = jnp.where(diag | (r < 2), 0, 4 * chip_hops + off_line)
 
     def step(n, carry):
         @pl.when((n < CHUNKS) & (r >= 2))

time: 43.7 us -> 42.1 us (0.963)
  Pallas kernels: 42.6 us -> 40.9 us
    pallas_call x1, Pallas kernels: 42.6 us -> 40.9 us  [body(): pl.pallas_call(functools.partial(kernel, (rows, cols, subs, order, width,...]
where the time goes in v4:
time: 42.1 us; the launch traced here: 41.9 us
  Pallas kernels  40.9 us (97%)
  local copies, waits for them, and re-layouts  0.97 us (2%)
    pallas_call x1, Pallas kernels, body(): pl.pallas_call(functools.partial(kernel, (rows, cols, subs, order, width,...  40.9 us
    unnamed x1, local copies, waits for them, and re-layouts  0.97 us

profile of v4, /device:TPU:29, one launch (start us, length us, event | category | flops | bytes accessed | tf_op | source)
XLA Modules:
  0.0 41.9 jit_solution(4907806535709155399)
XLA Ops:
  0.0 40.9 %shard_map.73 = f32[512,512]{1,0:T(8,128)S(1)} custom-call(bf16[1,4,1024,1024]{3,2,1,0:T(8,128)(2,1)} %inv_hbm.1, bf16[1,4,1024,256]{3,2,1,0:T(8,128)(2,1)} %cpl_hbm.1, s32[1,4]{1,0:T(1,128)} %orders.1, s32[4,1,4]{2,1,0:T(1,128)} %bitcast.7, s32[4,2,4]{2,1,0:T(2,128)} %bitcast.5, f32[512,512]{1,0:T(8,128)} %slab_hbm.1, f32[8,128]{1,0:T(8,128)} %bitcast.6), custom_call_target="tpu_custom_call" | custom-call | tf_op jit(solution)/shard_map/pallas_call | solution.py:308
  41.0 1.0 %copy.10 = f32[512,512]{1,0:T(8,128)} copy(f32[512,512]{1,0:T(8,128)S(1)} %shard_map.73) | data formatting | bytes 2097152

commit v5 on v4

--- a/solution.py
+++ b/solution.py
@@ -22,7 +22,7 @@
     dims,
     inv_hbm, cpl_hbm, orders, owners, offsets, slab_hbm, pivots,
     out,
-    a_buf, m_buf, slab, mm, sol, tiles, send, recv, placed, panel, left, piv,
+    a_buf, m_buf, slab, mm, sol, send, recv, placed, panel, left, piv,
     a_sem, m_sem, s_sem, t_send, t_recv, ax_send, ay_send, g_recv,
     up_send, dn_send, core_send, l_recv,
 ):
@@ -87,24 +87,6 @@
             placed[t, k * (nb + 1) + nb] = jnp.zeros((unit, unit), BF16)
             placed[t, nb * (nb + 1) + k] = jnp.zeros((unit, unit), BF16)
 
-    for s in range(subs):
-        load_m(s).wait()
-        live = lax.broadcasted_iota(jnp.int32, (order, width), 0) < orders[0, s]
-        mm[...] = jnp.where(live, m_buf[s], jnp.zeros((order, width), BF16))
-        for i in range(ablocks):
-            load_a(s, i).wait()
-            lo = i * AB
-            half = a_buf[s, lo:lo + AB, lo:lo + AB] * jnp.asarray(0.5, BF16)
-            part = jnp.dot(half, mm[lo:lo + AB], preferred_element_type=F32)
-            if i + 1 < ablocks:
-                part = part + jnp.dot(a_buf[s, lo:lo + AB, lo + AB:], mm[lo + AB:],
-                                      preferred_element_type=F32)
-            sol[lo:lo + AB] = part.astype(BF16)
-        half_tile = contract0(mm[...], sol[...])
-        whole_tile = (half_tile + jnp.transpose(half_tile)).astype(BF16)
-        for k, (a, b) in enumerate(pairs):
-            tiles[s, k] = whole_tile[a * unit:(a + 1) * unit, b * unit:(b + 1) * unit]
-
     neighbours = rows + jnp.where(q + 1 < chips, 1, 0) + jnp.where(q > 0, 1, 0)
     pl.semaphore_wait(barrier, neighbours)
 
@@ -121,9 +103,27 @@
             send_sem=t_send.at[t], recv_sem=t_recv.at[src_row],
             device_id=(t, c), device_id_type=MESH)
 
+    for s in range(subs):
+        load_m(s).wait()
+        for i in range(ablocks):
+            load_a(s, i).wait()
+
     for t in range(rows):
         _, which = pick(r, t)
-        value = tiles[which]
+        live = lax.broadcasted_iota(jnp.int32, (order, width), 0) < orders[0, which]
+        mm[...] = jnp.where(live, m_buf[which], jnp.zeros((order, width), BF16))
+        for i in range(ablocks):
+            lo = i * AB
+            half = a_buf[which, lo:lo + AB, lo:lo + AB] * jnp.asarray(0.5, BF16)
+            part = jnp.dot(half, mm[lo:lo + AB], preferred_element_type=F32)
+            if i + 1 < ablocks:
+                part = part + jnp.dot(a_buf[which, lo:lo + AB, lo + AB:], mm[lo + AB:],
+                                      preferred_element_type=F32)
+            sol[lo:lo + AB] = part.astype(BF16)
+        half_tile = contract0(mm[...], sol[...])
+        whole_tile = (half_tile + jnp.transpose(half_tile)).astype(BF16)
+        value = jnp.stack([whole_tile[a * unit:(a + 1) * unit, b * unit:(b + 1) * unit]
+                           for a, b in pairs])
 
         @pl.when(t != r)
         def _():
@@ -316,7 +316,6 @@
             pltpu.VMEM((tile, tile), F32),
             pltpu.VMEM((order, width), BF16),
             pltpu.VMEM((order, width), BF16),
-            pltpu.VMEM((subs, upper, unit, unit), BF16),
             pltpu.VMEM((rows, upper, unit, unit), BF16),
             pltpu.VMEM((rows, upper, unit, unit), BF16),
             pltpu.VMEM((rows, (nb + 1) * (nb + 1), unit, unit), BF16),

time: 42.1 us -> 38.3 us (0.910)
  Pallas kernels: 40.9 us -> 37.1 us
    pallas_call x1, Pallas kernels: 40.9 us -> 37.1 us  [body(): pl.pallas_call(functools.partial(kernel, (rows, cols, subs, order, width,...]
where the time goes in v5:
time: 38.3 us; the launch traced here: 38.1 us
  Pallas kernels  37.1 us (97%)
  local copies, waits for them, and re-layouts  0.97 us (3%)
    pallas_call x1, Pallas kernels, body(): pl.pallas_call(functools.partial(kernel, (rows, cols, subs, order, width,...  37.1 us
    unnamed x1, local copies, waits for them, and re-layouts  0.97 us

profile of v5, /device:TPU:29, one launch (start us, length us, event | category | flops | bytes accessed | tf_op | source)
XLA Modules:
  0.0 38.1 jit_solution(628232208084186272)
XLA Ops:
  0.0 37.1 %shard_map.73 = f32[512,512]{1,0:T(8,128)S(1)} custom-call(bf16[1,4,1024,1024]{3,2,1,0:T(8,128)(2,1)} %inv_hbm.1, bf16[1,4,1024,256]{3,2,1,0:T(8,128)(2,1)} %cpl_hbm.1, s32[1,4]{1,0:T(1,128)} %orders.1, s32[4,1,4]{2,1,0:T(1,128)} %bitcast.7, s32[4,2,4]{2,1,0:T(2,128)} %bitcast.5, f32[512,512]{1,0:T(8,128)} %slab_hbm.1, f32[8,128]{1,0:T(8,128)} %bitcast.6), custom_call_target="tpu_custom_call" | custom-call | tf_op jit(solution)/shard_map/pallas_call | solution.py:308
  37.1 1.0 %copy.10 = f32[512,512]{1,0:T(8,128)} copy(f32[512,512]{1,0:T(8,128)S(1)} %shard_map.73) | data formatting | bytes 2097152
